TPU v7x, 256 devices: a whole 4x4x8 slice. The times are simulated.
256 devices in a mesh: sub: 32 (over z, x), agg: 8 (over y, core).
Axes of the slice: x: 4, y: 4, z: 8, core: 2. Of those that a mesh axis runs over, the one named last changes fastest.
Arguments:
- dual_load: float32 [8, 32, 64, 1536], P('agg', 'sub'), may hold values from -58 to 58
- interface_inverse: bfloat16 [8, 32, 1536, 1536], P('agg', 'sub'), may hold values from -1 to 2.5, as said below
- dirichlet: bfloat16 [8, 32, 1536, 1536], P('agg', 'sub'), may hold values from -1 to 2.5, as said below
- coupling: bfloat16 [8, 32, 128, 1536], P('agg', 'sub'), may hold values from -0.15625 to 0.15625
- neighbours: int32 [8, 32, 8], P('agg', 'sub'), may hold values from -1 to 31, as said below
- face_counts: int32 [8, 32, 8], P('agg', 'sub'), may hold values from 0 to 192, as said below
- owners: int32 [8, 32, 128, 1], P('agg', 'sub'), may hold values from 0 to 7; in each aligned block of 128 rows (0 to 127, 128 to 255, ..., all dimensions but the last counted through in order) at most 48 rows name the same one
- primal_rows: int32 [8, 32, 128], P('agg', 'sub'), may hold values from 0 to 1023
- coarse_inverse: float32 [8, 1024, 1024], P('agg', 'sub'), may hold values from -1 to 1.5, as said below
Outputs:
- solution: float32 [8, 32, 64, 1536], P('agg', 'sub')
- residual: float32 [8, 32, 64, 1536], P('agg', 'sub')
Inputs may be any that keep to these rules, and one draw needn't show every extreme that they name: `neighbours`: each subdomain lists peers of its own aggregate by their index along sub, -1 in empty slots; no peer twice; if j lists i then i lists j; every listed peer lies within a cyclic distance of 4 along sub. `face_counts`: 0 exactly in empty slots, 48 or more elsewhere; both sides of a face give the same count and hold its rows in the same order. `owners`: among the 128 primal rows of one subdomain no aggregate is named more than 48 times. `interface_inverse`: each subdomain's matrix is symmetric positive definite. `dirichlet`: each subdomain's matrix is symmetric positive definite. `coarse_inverse`: each aggregate's matrix is symmetric positive definite.
All inputs are finite; a program needn't handle non-finite values.
Results may differ from a plain program's by a relative error of at most 0.011.
Values sent between devices are 32-bit elements; how exact they have to be, the bound alone decides.
No kernel may reach another device: no remote copies, remote signals or barrier semaphores. Data moves between devices by JAX's collectives and lax.ppermute only.
A program may use at most 128 MiB of HBM per device.

v0:
```python
import jax
import jax.numpy as jnp
from jax import lax
from jax.sharding import PartitionSpec as P

NC = 1024
CAP = 48
ITERS = 2
FULL_PRECISION = lax.Precision.HIGHEST
CONTRACT_LAST = (((1,), (1,)), ((), ()))


def from_behind_2(block, axis, distance):
    devices = range(lax.axis_size(axis))
    route = [((i - distance) % len(devices), i) for i in devices]
    return lax.ppermute(block, axis, route)


def shards(
    dual_load,
    interface_inverse,
    dirichlet,
    coupling,
    neighbours,
    face_counts,
    owners,
    primal_rows,
    coarse_inverse,
):
    inverse_block = interface_inverse[0, 0]
    dirichlet_block = dirichlet[0, 0]
    coupling_block = coupling[0, 0]
    peer_list = neighbours[0, 0]
    count_list = face_counts[0, 0]
    sub_count = lax.axis_size("sub")
    agg_count = lax.axis_size("agg")
    position = lax.axis_index("sub")
    slot_count = peer_list.shape[0]
    inner_order = inverse_block.shape[0]
    face_depth = inner_order // slot_count
    reach = min(4, (sub_count - 1) // 2)
    inside = (
        (jnp.arange(face_depth, dtype=jnp.int32)[None, :] < count_list[:, None])
        .reshape(1, inner_order)
        .astype(jnp.float32)
    )

    def assemble(local):
        case_count = local.shape[0]
        faces = local.reshape(case_count, slot_count, face_depth)
        placed = jnp.zeros_like(faces)
        for distance in range(1, reach + 1):
            ahead = (position + distance) % sub_count
            behind = (position + sub_count - distance) % sub_count
            to_ahead = (peer_list == ahead).astype(jnp.float32)[None, :, None]
            to_behind = (peer_list == behind).astype(jnp.float32)[None, :, None]
            upward = jnp.sum(faces * to_ahead, axis=1)
            downward = jnp.sum(faces * to_behind, axis=1)
            from_behind = from_behind_2(upward, "sub", distance)
            from_ahead = from_behind_2(downward, "sub", -distance)
            placed = (
                placed + to_behind * from_behind[:, None, :] + to_ahead * from_ahead[:, None, :]
            )
        return inside * (local + placed.reshape(case_count, inner_order))

    owner_ids = owners[0, 0, :, 0]
    row_ids = primal_rows[0, 0]
    owner_hot = (owner_ids[:, None] == jnp.arange(agg_count, dtype=jnp.int32)[None, :]).astype(
        jnp.int32
    )
    earlier = jnp.cumsum(owner_hot, axis=0) - owner_hot
    owner_rank = jnp.sum(earlier * owner_hot, axis=1)
    slot_index = owner_ids * CAP + owner_rank
    packing = slot_index[:, None] == jnp.arange(agg_count * CAP, dtype=jnp.int32)[None, :]
    packing_float = packing.astype(jnp.float32)
    sent_rows = jnp.sum(packing.astype(jnp.int32) * (row_ids[:, None] + 1), axis=0) - 1
    got_rows = lax.all_to_all(sent_rows, "agg", split_axis=0, concat_axis=0, tiled=True)
    scatter_hot = (got_rows[:, None] == jnp.arange(NC, dtype=jnp.int32)[None, :]).astype(
        jnp.float32
    )
    inverse_rows = coarse_inverse[0]

    def precondition(field):
        packed = field.astype(jnp.bfloat16)
        return assemble(
            inside * jnp.dot(packed, dirichlet_block, preferred_element_type=jnp.float32)
        )

    def residual_norm(first, second):
        return lax.psum(jnp.sum(first * second, axis=1), ("sub", "agg"))

    rhs = assemble(inside * dual_load[0, 0])
    solution = jnp.zeros_like(rhs)
    residual = rhs
    precond = precondition(residual)
    direction = precond
    residual_dot = residual_norm(residual, precond)
    for iteration in range(ITERS):
        operator_packed = direction.astype(jnp.bfloat16)
        own = jnp.dot(operator_packed, inverse_block, preferred_element_type=jnp.float32)
        terms = lax.dot_general(
            operator_packed, coupling_block, CONTRACT_LAST, preferred_element_type=jnp.float32
        )
        outgoing = jnp.dot(terms, packing_float, precision=FULL_PRECISION)
        gathered = jnp.dot(
            lax.all_to_all(outgoing, "agg", split_axis=1, concat_axis=1, tiled=True),
            scatter_hot,
            precision=FULL_PRECISION,
        )
        coarse_rhs = lax.psum(gathered, "sub")
        partial_rows = lax.dot_general(
            coarse_rhs, inverse_rows, CONTRACT_LAST, precision=FULL_PRECISION
        )
        coarse_sol = lax.all_gather(partial_rows, "sub", axis=1, tiled=True)
        answer = lax.dot_general(coarse_sol, scatter_hot, CONTRACT_LAST, precision=FULL_PRECISION)
        returned = lax.all_to_all(answer, "agg", split_axis=1, concat_axis=1, tiled=True)
        local_back = lax.dot_general(
            returned, packing_float, CONTRACT_LAST, precision=FULL_PRECISION
        )
        correction = jnp.dot(
            local_back.astype(jnp.bfloat16), coupling_block, preferred_element_type=jnp.float32
        )
        image = assemble(inside * (own + correction))
        alpha = (residual_dot / lax.psum(jnp.sum(direction * image, axis=1), ("sub", "agg")))[
            :, None
        ]
        solution = solution + alpha * direction
        residual = residual - alpha * image
        if iteration + 1 < ITERS:
            precond = precondition(residual)
            next_dot = residual_norm(residual, precond)
            direction = precond + (next_dot / residual_dot)[:, None] * direction
            residual_dot = next_dot
    return (solution[None, None], residual[None, None])


def solution(mesh):
    in_specs = (
        P("agg", "sub", None, None),
        P("agg", "sub", None, None),
        P("agg", "sub", None, None),
        P("agg", "sub", None, None),
        P("agg", "sub", None),
        P("agg", "sub", None),
        P("agg", "sub", None, None),
        P("agg", "sub", None),
        P("agg", "sub", None),
    )
    out_specs = (P("agg", "sub", None, None), P("agg", "sub", None, None))
    return jax.shard_map(shards, mesh=mesh, in_specs=in_specs, out_specs=out_specs, check_vma=False)
```

profile of v0, /device:TPU:1, one launch (start us, length us, event | category | flops | bytes accessed | tf_op | source)
XLA Modules:
  0.0 917.8 jit_solution(6425770265424465426)
XLA Ops:
  11.5 2.1 collective-permute-start
  13.6 6.6 collective-permute-start.1
  20.4 2.7 collective-permute-start.7
  26.0 2.5 collective-permute-start.2
  28.4 2.6 collective-permute-start.3
  50.8 5.2 fusion.8
  56.0 2.0 reshape.646
  58.0 2.5 multiply_reduce_fusion.31
  60.5 4.7 collective-permute-start.11
  65.2 2.7 collective-permute-start.9
  76.5 10.1 %all-to-all-start.1 = ((s32[8,48,1]{1,2,0:T(1,128)}), s32[8,48,1]{1,2,0:T(1,128)}, u32[]{:S(2)}, u32[]{:S(2)}) async-start(s32[8,48,1]{1,2,0:T(1,128)} %bitcast.111), calls=%async_computation.1 | async-start | bytes 8192 | tf_op jit(solution)/shard_map/all_to_all | solution.py:77
  108.6 2.0 mul.1287
  111.4 2.0 mul.1259
  113.4 2.3 add_multiply_fusion.3
  119.4 4.8 all-to-all-start
  129.8 2.4 reduce.4
  133.9 2.4 fusion.29
  136.4 138.3 %all-reduce.4.cloned.1.call-done = f32[64,1024]{1,0:T(8,128)} async-done(((f32[64,1024]{1,0:T(8,128)}), f32[64,1024]{1,0:T(8,128)}) %all-reduce.4.cloned.1.call-update) | async-done | bytes 262160 | tf_op jit(solution)/shard_map/psum | solution.py:110
  275.9 35.9 %all_gather.6 = f32[64,1024]{0,1:T(8,128)S(1)} all-gather(f32[64,32]{0,1:T(8,128)S(1)} %fusion.58), channel_id=1, replica_groups=mesh['sub'=32,'agg'=8] {'sub'}, dimensions={1}, use_global_device_ids=true | all-gather | bytes 270336 | tf_op jit(solution)/shard_map/all_gather | solution.py:114
  311.8 2.3 fusion.28
  315.8 26.7 %all_to_all.54 = f32[8,1,3072]{2,1,0:T(1,128)} all-to-all(f32[8,1,3072]{2,1,0:T(1,128)} %reshape.670), channel_id=1, replica_groups=mesh['sub'=32,'agg'=8] {'agg'}, dimensions={0} | all-to-all | bytes 196608 | tf_op jit(solution)/shard_map/all_to_all | solution.py:116
  342.5 2.4 reduce.5
  348.1 4.0 fusion.23
  352.1 2.0 reshape.647
  354.1 3.2 multiply_reduce_fusion.23
  357.3 2.0 collective-permute-start.19
  360.2 4.5 collective-permute-start.17
  364.7 3.8 collective-permute-start.21
  368.5 2.7 collective-permute-start.23
  394.4 3.9 multiply_reduce_fusion.42
  398.5 77.6 %all-reduce = (f32[64]{0:T(128)S(1)}, f32[64]{0:T(128)S(1)}) all-reduce(f32[64]{0:T(128)S(1)} %get-tuple-element.43, f32[64]{0:T(128)S(1)} %get-tuple-element.42), channel_id=1, replica_groups=mesh['sub'=32,'agg'=8] {'sub','agg'}, use_global_device_ids=true, to_apply=%region_17.18 | all-reduce | flops 128 | bytes 1024 | tf_op jit(solution)/shard_map/psum | solution.py:90
  477.2 3.3 fusion.11
  483.4 2.2 collective-permute-start.26
  485.6 2.5 collective-permute-start.25
  488.2 3.5 collective-permute-start.29
  491.7 2.7 collective-permute-start.31
  505.9 77.6 %psum.45 = f32[64]{0:T(128)S(1)} all-reduce(f32[64]{0:T(128)S(1)} %get-tuple-element.48), channel_id=1, replica_groups=mesh['sub'=32,'agg'=8] {'sub','agg'}, use_global_device_ids=true, to_apply=%region_41.42 | all-reduce | flops 64 | bytes 512 | tf_op jit(solution)/shard_map/psum | solution.py:90
  585.7 8.1 all_to_all.55
  596.3 136.3 %all-reduce.6.cloned.1.call-done = f32[64,1024]{1,0:T(8,128)} async-done(((f32[64,1024]{1,0:T(8,128)}), f32[64,1024]{1,0:T(8,128)}) %all-reduce.6.cloned.1.call-update) | async-done | bytes 262160 | tf_op jit(solution)/shard_map/psum | solution.py:110
  733.9 35.9 %all_gather.7 = f32[64,1024]{0,1:T(8,128)S(1)} all-gather(f32[64,32]{0,1:T(8,128)S(1)} %fusion.56), channel_id=1, replica_groups=mesh['sub'=32,'agg'=8] {'sub'}, dimensions={1}, use_global_device_ids=true | all-gather | bytes 270336 | tf_op jit(solution)/shard_map/all_gather | solution.py:114
  770.8 26.7 %all_to_all.56 = f32[8,1,3072]{2,1,0:T(1,128)S(1)} all-to-all(f32[8,1,3072]{2,1,0:T(1,128)S(1)} %reshape.674), channel_id=1, replica_groups=mesh['sub'=32,'agg'=8] {'agg'}, dimensions={0} | all-to-all | bytes 196608 | tf_op jit(solution)/shard_map/all_to_all | solution.py:116
  799.1 3.3 fusion.20
  804.3 2.0 collective-permute-start.35
  807.2 4.5 collective-permute-start.33
  811.7 3.6 collective-permute-start.37
  815.3 2.7 collective-permute-start.39
  829.3 2.0 multiply_reduce_fusion.40
  831.3 77.7 %psum.47 = f32[64]{0:T(128)S(1)} all-reduce(f32[64]{0:T(128)S(1)} %get-tuple-element.46), channel_id=1, replica_groups=mesh['sub'=32,'agg'=8] {'sub','agg'}, use_global_device_ids=true, to_apply=%region_52.53 | all-reduce | flops 64 | bytes 512 | tf_op jit(solution)/shard_map/psum | solution.py:124
  (331 shorter events, 139.2 us)
Async XLA Ops:
  7.2 108.6 %copy-start = (bf16[1,1,128,1536]{3,2,1,0:T(8,128)(2,1)S(1)}, bf16[1,1,128,1536]{3,2,1,0:T(8,128)(2,1)}, u32[]{:S(2)}) copy-start(bf16[1,1,128,1536]{3,2,1,0:T(8,128)(2,1)} %param.12) | copy-start | bytes 1179652
  11.5 35.6 %collective-permute-start = (f32[64,192]{1,0:T(8,128)S(1)}, f32[64,192]{1,0:T(8,128)}, u32[]{:S(2)}, u32[]{:S(2)}) collective-permute-start(f32[64,192]{1,0:T(8,128)S(1)} %get-tuple-element.2), channel_id=1, source_target_pairs={{248,0},{0,8},{8,16},{16,24},{24,32},{32,40},{40,48},{48,56},{56,6... | collective-permute-start | bytes 147464 | tf_op jit(solution)/shard_map/ppermute | solution.py:16
  13.6 29.9 %collective-permute-start.1 = (f32[64,192]{1,0:T(8,128)}, f32[64,192]{1,0:T(8,128)}, u32[]{:S(2)}, u32[]{:S(2)}) collective-permute-start(f32[64,192]{1,0:T(8,128)} %get-tuple-element.3), channel_id=1, source_target_pairs={{8,0},{16,8},{24,16},{32,24},{40,32},{48,40},{56,48},{64,56},{72,6... | collective-permute-start | bytes 147464 | tf_op jit(solution)/shard_map/ppermute | solution.py:16
  20.3 5.7 collective-permute-start.5
  20.4 8.1 collective-permute-start.6
  20.4 10.7 %collective-permute-start.7 = (f32[64,192]{1,0:T(8,128)S(1)}, f32[64,192]{1,0:T(8,128)S(1)}, u32[]{:S(2)}, u32[]{:S(2)}) collective-permute-start(f32[64,192]{1,0:T(8,128)S(1)} %get-tuple-element.9), channel_id=1, source_target_pairs={{32,0},{40,8},{48,16},{56,24},{64,32},{72,40},{80,48},{88,56},{96,... | collective-permute-start | bytes 147464 | tf_op jit(solution)/shard_map/ppermute | solution.py:16
  26.0 13.9 %collective-permute-start.2 = (f32[64,192]{1,0:T(8,128)}, f32[64,192]{1,0:T(8,128)}, u32[]{:S(2)}, u32[]{:S(2)}) collective-permute-start(f32[64,192]{1,0:T(8,128)} %get-tuple-element.4), channel_id=1, source_target_pairs={{240,0},{248,8},{0,16},{8,24},{16,32},{24,40},{32,48},{40,56},{48,... | collective-permute-start | bytes 147464 | tf_op jit(solution)/shard_map/ppermute | solution.py:16
  28.4 9.6 %collective-permute-start.3 = (f32[64,192]{1,0:T(8,128)S(1)}, f32[64,192]{1,0:T(8,128)}, u32[]{:S(2)}, u32[]{:S(2)}) collective-permute-start(f32[64,192]{1,0:T(8,128)S(1)} %get-tuple-element.5), channel_id=1, source_target_pairs={{16,0},{24,8},{32,16},{40,24},{48,32},{56,40},{64,48},{72,56},{80,... | collective-permute-start | bytes 147464 | tf_op jit(solution)/shard_map/ppermute | solution.py:16
  31.1 6.0 collective-permute-start.4
  60.5 8.4 collective-permute-start.11
  65.2 6.7 collective-permute-start.10
  65.2 8.3 collective-permute-start.9
  68.6 41.9 %collective-permute-start.8 = (f32[64,192]{1,0:T(8,128)S(1)}, f32[64,192]{1,0:T(8,128)S(1)}, u32[]{:S(2)}, u32[]{:S(2)}) collective-permute-start(f32[64,192]{1,0:T(8,128)S(1)} %get-tuple-element.34), channel_id=1, source_target_pairs={{248,0},{0,8},{8,16},{16,24},{24,32},{32,40},{40,48},{48,56},{56,6... | collective-permute-start | bytes 147464 | tf_op jit(solution)/shard_map/ppermute | solution.py:16
  68.7 39.0 %collective-permute-start.15 = (f32[64,192]{1,0:T(8,128)S(1)}, f32[64,192]{1,0:T(8,128)S(1)}, u32[]{:S(2)}, u32[]{:S(2)}) collective-permute-start(f32[64,192]{1,0:T(8,128)S(1)} %get-tuple-element.35), channel_id=1, source_target_pairs={{32,0},{40,8},{48,16},{56,24},{64,32},{72,40},{80,48},{88,56},{96,... | collective-permute-start | bytes 147464 | tf_op jit(solution)/shard_map/ppermute | solution.py:16
  68.8 35.2 %collective-permute-start.14 = (f32[64,192]{1,0:T(8,128)S(1)}, f32[64,192]{1,0:T(8,128)}, u32[]{:S(2)}, u32[]{:S(2)}) collective-permute-start(f32[64,192]{1,0:T(8,128)S(1)} %get-tuple-element.36), channel_id=1, source_target_pairs={{224,0},{232,8},{240,16},{248,24},{0,32},{8,40},{16,48},{24,56},{3... | collective-permute-start | bytes 147464 | tf_op jit(solution)/shard_map/ppermute | solution.py:16
  71.9 28.5 %collective-permute-start.13 = (f32[64,192]{1,0:T(8,128)S(1)}, f32[64,192]{1,0:T(8,128)}, u32[]{:S(2)}, u32[]{:S(2)}) collective-permute-start(f32[64,192]{1,0:T(8,128)S(1)} %get-tuple-element.37), channel_id=1, source_target_pairs={{24,0},{32,8},{40,16},{48,24},{56,32},{64,40},{72,48},{80,56},{88,... | collective-permute-start | bytes 147464 | tf_op jit(solution)/shard_map/ppermute | solution.py:16
  73.5 23.3 %collective-permute-start.12 = (f32[64,192]{1,0:T(8,128)S(1)}, f32[64,192]{1,0:T(8,128)}, u32[]{:S(2)}, u32[]{:S(2)}) collective-permute-start(f32[64,192]{1,0:T(8,128)S(1)} %get-tuple-element.38), channel_id=1, source_target_pairs={{232,0},{240,8},{248,16},{0,24},{8,32},{16,40},{24,48},{32,56},{40... | collective-permute-start | bytes 147464 | tf_op jit(solution)/shard_map/ppermute | solution.py:16
  76.5 42.9 %all-to-all-start.1 = ((s32[8,48,1]{1,2,0:T(1,128)}), s32[8,48,1]{1,2,0:T(1,128)}, u32[]{:S(2)}, u32[]{:S(2)}) async-start(s32[8,48,1]{1,2,0:T(1,128)} %bitcast.111), calls=%async_computation.1 | async-start | bytes 8192 | tf_op jit(solution)/shard_map/all_to_all | solution.py:77
  108.6 166.1 %copy-start.9 = (f32[1,32,1024]{2,1,0:T(8,128)S(1)}, f32[1,32,1024]{2,1,0:T(8,128)}, u32[]{:S(2)}) copy-start(f32[1,32,1024]{2,1,0:T(8,128)} %param.17) | copy-start | bytes 393220
  119.4 9.9 %all-to-all-start = ((f32[8,1,3072]{2,1,0:T(1,128)}), f32[8,1,3072]{2,1,0:T(1,128)}, u32[]{:S(2)}, u32[]{:S(2)}) async-start(f32[8,1,3072]{2,1,0:T(1,128)} %reshape.668), calls=%async_computation | async-start | bytes 196608 | tf_op jit(solution)/shard_map/all_to_all | solution.py:106
  124.2 150.4 %all-reduce.4.cloned.1.call-start = ((), (), s32[]{:S(2)}) async-start(), calls=%async_computation.5 | async-start | bytes 524288 | tf_op jit(solution)/shard_map/psum | solution.py:110
  136.3 596.3 %all-reduce.6.cloned.1.call-start = ((), (), s32[]{:S(2)}) async-start(), calls=%async_computation.6 | async-start | bytes 524288 | tf_op jit(solution)/shard_map/psum | solution.py:110
  357.3 11.3 %collective-permute-start.19 = (f32[64,192]{1,0:T(8,128)S(1)}, f32[64,192]{1,0:T(8,128)}, u32[]{:S(2)}, u32[]{:S(2)}) collective-permute-start(f32[64,192]{1,0:T(8,128)S(1)} %get-tuple-element.31), channel_id=1, source_target_pairs={{16,0},{24,8},{32,16},{40,24},{48,32},{56,40},{64,48},{72,56},{80,... | collective-permute-start | bytes 147464 | tf_op jit(solution)/shard_map/ppermute | solution.py:16
  359.2 9.3 %collective-permute-start.18 = (f32[64,192]{1,0:T(8,128)S(1)}, f32[64,192]{1,0:T(8,128)}, u32[]{:S(2)}, u32[]{:S(2)}) collective-permute-start(f32[64,192]{1,0:T(8,128)S(1)} %get-tuple-element.32), channel_id=1, source_target_pairs={{240,0},{248,8},{0,16},{8,24},{16,32},{24,40},{32,48},{40,56},{48,... | collective-permute-start | bytes 147464 | tf_op jit(solution)/shard_map/ppermute | solution.py:16
  360.2 11.0 %collective-permute-start.17 = (f32[64,192]{1,0:T(8,128)S(1)}, f32[64,192]{1,0:T(8,128)}, u32[]{:S(2)}, u32[]{:S(2)}) collective-permute-start(f32[64,192]{1,0:T(8,128)S(1)} %get-tuple-element.33), channel_id=1, source_target_pairs={{8,0},{16,8},{24,16},{32,24},{40,32},{48,40},{56,48},{64,56},{72,6... | collective-permute-start | bytes 147464 | tf_op jit(solution)/shard_map/ppermute | solution.py:16
  364.7 20.5 %collective-permute-start.20 = (f32[64,192]{1,0:T(8,128)}, f32[64,192]{1,0:T(8,128)}, u32[]{:S(2)}, u32[]{:S(2)}) collective-permute-start(f32[64,192]{1,0:T(8,128)} %get-tuple-element.30), channel_id=1, source_target_pairs={{232,0},{240,8},{248,16},{0,24},{8,32},{16,40},{24,48},{32,56},{40... | collective-permute-start | bytes 147464 | tf_op jit(solution)/shard_map/ppermute | solution.py:16
  364.7 22.3 %collective-permute-start.21 = (f32[64,192]{1,0:T(8,128)}, f32[64,192]{1,0:T(8,128)}, u32[]{:S(2)}, u32[]{:S(2)}) collective-permute-start(f32[64,192]{1,0:T(8,128)} %get-tuple-element.29), channel_id=1, source_target_pairs={{24,0},{32,8},{40,16},{48,24},{56,32},{64,40},{72,48},{80,56},{88,... | collective-permute-start | bytes 147464 | tf_op jit(solution)/shard_map/ppermute | solution.py:16
  368.5 20.4 %collective-permute-start.22 = (f32[64,192]{1,0:T(8,128)}, f32[64,192]{1,0:T(8,128)}, u32[]{:S(2)}, u32[]{:S(2)}) collective-permute-start(f32[64,192]{1,0:T(8,128)} %get-tuple-element.28), channel_id=1, source_target_pairs={{224,0},{232,8},{240,16},{248,24},{0,32},{8,40},{16,48},{24,56},{3... | collective-permute-start | bytes 147464 | tf_op jit(solution)/shard_map/ppermute | solution.py:16
  368.5 22.2 %collective-permute-start.23 = (f32[64,192]{1,0:T(8,128)}, f32[64,192]{1,0:T(8,128)}, u32[]{:S(2)}, u32[]{:S(2)}) collective-permute-start(f32[64,192]{1,0:T(8,128)} %get-tuple-element.27), channel_id=1, source_target_pairs={{32,0},{40,8},{48,16},{56,24},{64,32},{72,40},{80,48},{88,56},{96,... | collective-permute-start | bytes 147464 | tf_op jit(solution)/shard_map/ppermute | solution.py:16
  371.2 21.3 %collective-permute-start.16 = (f32[64,192]{1,0:T(8,128)}, f32[64,192]{1,0:T(8,128)}, u32[]{:S(2)}, u32[]{:S(2)}) collective-permute-start(f32[64,192]{1,0:T(8,128)} %get-tuple-element.26), channel_id=1, source_target_pairs={{248,0},{0,8},{8,16},{16,24},{24,32},{32,40},{40,48},{48,56},{56,6... | collective-permute-start | bytes 147464 | tf_op jit(solution)/shard_map/ppermute | solution.py:16
  482.7 9.0 collective-permute-start.27
  483.4 8.2 collective-permute-start.26
  485.6 8.7 collective-permute-start.25
  488.1 6.9 collective-permute-start.28
  488.2 8.7 collective-permute-start.29
  491.7 7.0 collective-permute-start.30
  491.7 8.8 collective-permute-start.31
  494.4 7.9 collective-permute-start.24
  504.1 294.4 %copy-start.51 = (s32[128]{0:T(128)S(1)}, s32[128]{0:T(128)}, u32[]{:S(2)}) copy-start(s32[128]{0:T(128)} %multiply_add_fusion.1) | copy-start | bytes 1540
  583.5 218.8 %copy-start.54 = (f32[64]{0:T(128)}, f32[64]{0:T(128)S(1)}, u32[]{:S(2)}) copy-start(f32[64]{0:T(128)S(1)} %psum.45) | copy-start | bytes 772
  804.3 11.0 %collective-permute-start.35 = (f32[64,192]{1,0:T(8,128)S(1)}, f32[64,192]{1,0:T(8,128)S(1)}, u32[]{:S(2)}, u32[]{:S(2)}) collective-permute-start(f32[64,192]{1,0:T(8,128)S(1)} %get-tuple-element.15), channel_id=1, source_target_pairs={{16,0},{24,8},{32,16},{40,24},{48,32},{56,40},{64,48},{72,56},{80,... | collective-permute-start | bytes 147464 | tf_op jit(solution)/shard_map/ppermute | solution.py:16
  806.2 9.1 collective-permute-start.34
  807.2 10.8 %collective-permute-start.33 = (f32[64,192]{1,0:T(8,128)S(1)}, f32[64,192]{1,0:T(8,128)S(1)}, u32[]{:S(2)}, u32[]{:S(2)}) collective-permute-start(f32[64,192]{1,0:T(8,128)S(1)} %get-tuple-element.17), channel_id=1, source_target_pairs={{8,0},{16,8},{24,16},{32,24},{40,32},{48,40},{56,48},{64,56},{72,6... | collective-permute-start | bytes 147464 | tf_op jit(solution)/shard_map/ppermute | solution.py:16
  811.7 8.5 collective-permute-start.36
  811.7 10.3 %collective-permute-start.37 = (f32[64,192]{1,0:T(8,128)}, f32[64,192]{1,0:T(8,128)}, u32[]{:S(2)}, u32[]{:S(2)}) collective-permute-start(f32[64,192]{1,0:T(8,128)} %get-tuple-element.13), channel_id=1, source_target_pairs={{24,0},{32,8},{40,16},{48,24},{56,32},{64,40},{72,48},{80,56},{88,... | collective-permute-start | bytes 147464 | tf_op jit(solution)/shard_map/ppermute | solution.py:16
  815.3 8.6 collective-permute-start.38
  815.3 10.3 %collective-permute-start.39 = (f32[64,192]{1,0:T(8,128)S(1)}, f32[64,192]{1,0:T(8,128)}, u32[]{:S(2)}, u32[]{:S(2)}) collective-permute-start(f32[64,192]{1,0:T(8,128)S(1)} %get-tuple-element.11), channel_id=1, source_target_pairs={{32,0},{40,8},{48,16},{56,24},{64,32},{72,40},{80,48},{88,56},{96,... | collective-permute-start | bytes 147464 | tf_op jit(solution)/shard_map/ppermute | solution.py:16
  818.0 9.5 %collective-permute-start.32 = (f32[64,192]{1,0:T(8,128)S(1)}, f32[64,192]{1,0:T(8,128)}, u32[]{:S(2)}, u32[]{:S(2)}) collective-permute-start(f32[64,192]{1,0:T(8,128)S(1)} %get-tuple-element.10), channel_id=1, source_target_pairs={{248,0},{0,8},{8,16},{16,24},{24,32},{32,40},{40,48},{48,56},{56,6... | collective-permute-start | bytes 147464 | tf_op jit(solution)/shard_map/ppermute | solution.py:16
  (52 other events, 1553.4 us)
Sparse Core Ops, SparseCore 0:
  136.4 138.1 all-reduce.3
  596.4 136.1 all-reduce.5
where the time goes:
time: 927 us; the launch traced here: 918 us
  blocking collectives  366 us (39%)
  waiting for transfers between devices  278 us (30%)
  local copies, waits for them, and re-layouts  105 us (11%)
  starting transfers between devices  83.3 us (9%)
  other arithmetic  39.7 us (4%)
  matrix products  30.5 us (3%)
  between operations  15.6 us (2%)
    psum x2, waiting for transfers between devices, shards(): coarse_rhs = lax.psum(gathered, 'sub')  275 us
    psum x2, blocking collectives, residual_norm(): return lax.psum(jnp.sum(first * second, axis=1), ('sub', 'agg'))  155 us
    psum x1, blocking collectives, shards(): lax.psum(jnp.sum(direction * image, axis=1), ('sub', 'agg'))  77.7 us
    all_gather x2, blocking collectives, shards(): coarse_sol = lax.all_gather(partial_rows, 'sub', axis=1, tiled=True)  71.7 us
    ppermute x40, starting transfers between devices, from_behind_2(): return lax.ppermute(block, axis, route)  68.3 us
    all_to_all x2, blocking collectives, shards(): lax.all_to_all(answer, 'agg', split_axis=1, concat_axis=1, tiled=True)  53.4 us
    mul x52, local copies, waits for them, and re-layouts, assemble(): to_behind * from_behind[:, None, :]  46.7 us
    mul x44, local copies, waits for them, and re-layouts, assemble(): to_ahead * from_ahead[:, None, :]  40.9 us
  transfers between devices with their start and end apart: 44, of which 4 were waited for; matrix products, arithmetic and copies ran while one was open for 10% of the time, Pallas kernels for 0%

commit v1 on v0

--- a/solution.py
+++ b/solution.py
@@ -121,9 +121,10 @@
             local_back.astype(jnp.bfloat16), coupling_block, preferred_element_type=jnp.float32
         )
         image = assemble(inside * (own + correction))
-        alpha = (residual_dot / lax.psum(jnp.sum(direction * image, axis=1), ("sub", "agg")))[
-            :, None
-        ]
+        alpha = (
+            residual_dot
+            / jnp.sum(lax.all_gather(jnp.sum(direction * image, axis=1), ("sub", "agg")), axis=0)
+        )[:, None]
         solution = solution + alpha * direction
         residual = residual - alpha * image
         if iteration + 1 < ITERS:

time: 927 us -> 1260 us (1.36)
  waiting for transfers between devices: 278 us -> 682 us
  blocking collectives: 366 us -> 289 us
    unnamed x2 -> x6, waiting for transfers between devices: 0.03 us -> 404 us
    psum x1 -> x0, blocking collectives: 77.7 us -> none  [shards(): lax.psum(jnp.sum(direction * image, axis=1), ('sub', 'agg'))]
  transfers between devices with their start and end apart: 44 -> 46, of which waited for: 4 -> 6; matrix products, arithmetic and copies ran while one was open for 10% -> 8% of each run, Pallas kernels for 0% -> 0%
where the time goes in v1:
time: 1260 us; the launch traced here: 1250 us
  waiting for transfers between devices  682 us (54%)
  blocking collectives  289 us (23%)
  local copies, waits for them, and re-layouts  109 us (9%)
  starting transfers between devices  84.7 us (7%)
  other arithmetic  39.2 us (3%)
  matrix products  30.6 us (2%)
  between operations  15.4 us (1%)
    unnamed x6, waiting for transfers between devices  404 us
    psum x2, waiting for transfers between devices, shards(): coarse_rhs = lax.psum(gathered, 'sub')  275 us
    psum x2, blocking collectives, residual_norm(): return lax.psum(jnp.sum(first * second, axis=1), ('sub', 'agg'))  156 us
    all_gather x2, blocking collectives, shards(): coarse_sol = lax.all_gather(partial_rows, 'sub', axis=1, tiled=True)  71.7 us
    ppermute x40, starting transfers between devices, from_behind_2(): return lax.ppermute(block, axis, route)  69.6 us
    all_to_all x2, blocking collectives, shards(): lax.all_to_all(answer, 'agg', split_axis=1, concat_axis=1, tiled=True)  53.4 us
    mul x52, local copies, waits for them, and re-layouts, assemble(): to_behind * from_behind[:, None, :]  46.7 us
    mul x44, local copies, waits for them, and re-layouts, assemble(): to_ahead * from_ahead[:, None, :]  40.9 us
  transfers between devices with their start and end apart: 46, of which 6 were waited for; matrix products, arithmetic and copies ran while one was open for 8% of the time, Pallas kernels for 0%

profile of v1, /device:TPU:1, one launch (start us, length us, event | category | flops | bytes accessed | tf_op | source)
XLA Modules:
  0.0 1249.8 jit_solution(7072752203422601458)
XLA Ops:
  11.5 2.1 collective-permute-start
  13.6 6.6 collective-permute-start.1
  20.4 2.7 collective-permute-start.7
  26.0 2.5 collective-permute-start.2
  28.4 2.6 collective-permute-start.3
  50.9 5.2 fusion.8
  56.0 2.0 reshape.646
  58.0 2.5 multiply_reduce_fusion.31
  60.5 4.7 collective-permute-start.11
  65.2 2.7 collective-permute-start.9
  76.6 10.2 all-to-all-start.1
  108.6 2.0 mul.1287
  111.5 2.0 mul.1259
  113.4 2.3 add_multiply_fusion.3
  119.5 4.8 all-to-all-start
  129.9 2.4 reduce.4
  133.9 2.4 fusion.29
  136.4 138.3 %all-reduce.7.cloned.1.call-done = f32[64,1024]{1,0:T(8,128)} async-done(((f32[64,1024]{1,0:T(8,128)}), f32[64,1024]{1,0:T(8,128)}) %all-reduce.7.cloned.1.call-update) | async-done | bytes 262160 | tf_op jit(solution)/shard_map/psum | solution.py:110
  276.0 35.9 %all_gather.18 = f32[64,1024]{0,1:T(8,128)S(1)} all-gather(f32[64,32]{0,1:T(8,128)S(1)} %fusion.58), channel_id=1, replica_groups=mesh['sub'=32,'agg'=8] {'sub'}, dimensions={1}, use_global_device_ids=true | all-gather | bytes 270336 | tf_op jit(solution)/shard_map/all_gather | solution.py:114
  311.9 2.3 fusion.28
  315.8 26.7 %all_to_all.54 = f32[8,1,3072]{2,1,0:T(1,128)} all-to-all(f32[8,1,3072]{2,1,0:T(1,128)} %reshape.676), channel_id=1, replica_groups=mesh['sub'=32,'agg'=8] {'agg'}, dimensions={0} | all-to-all | bytes 196608 | tf_op jit(solution)/shard_map/all_to_all | solution.py:116
  342.6 2.4 reduce.5
  348.1 4.0 fusion.23
  352.1 2.0 reshape.647
  354.1 3.2 multiply_reduce_fusion.23
  357.3 2.0 collective-permute-start.19
  360.3 4.5 collective-permute-start.17
  364.8 3.8 collective-permute-start.21
  368.6 2.7 collective-permute-start.23
  394.5 3.9 multiply_reduce_fusion.42
  399.5 78.1 %psum.28 = f32[64]{0:T(128)S(1)} all-reduce(f32[64]{0:T(128)S(1)} %get-tuple-element.43), channel_id=1, replica_groups=mesh['sub'=32,'agg'=8] {'sub','agg'}, use_global_device_ids=true, to_apply=%region_17.18 | all-reduce | flops 64 | bytes 512 | tf_op jit(solution)/shard_map/psum | solution.py:90
  477.6 162.8 %all-reduce.11.cloned.1.call-done = f32[16384]{0:T(1024)} async-done(((f32[16384]{0:T(1024)}), f32[16384]{0:T(1024)}) %all-reduce.11.cloned.1.call-update) | async-done | bytes 65552
  642.5 3.3 fusion.11
  650.9 3.7 collective-permute-start.25
  654.6 3.6 collective-permute-start.29
  658.2 2.7 collective-permute-start.31
  672.5 77.8 %psum.30 = f32[64]{0:T(128)S(1)} all-reduce(f32[64]{0:T(128)S(1)} %get-tuple-element.46), channel_id=1, replica_groups=mesh['sub'=32,'agg'=8] {'sub','agg'}, use_global_device_ids=true, to_apply=%region_41.42 | all-reduce | flops 64 | bytes 512 | tf_op jit(solution)/shard_map/psum | solution.py:90
  752.5 8.5 all_to_all.55
  763.4 137.0 %all-reduce.9.cloned.1.call-done = f32[64,1024]{1,0:T(8,128)} async-done(((f32[64,1024]{1,0:T(8,128)}), f32[64,1024]{1,0:T(8,128)}) %all-reduce.9.cloned.1.call-update) | async-done | bytes 262160 | tf_op jit(solution)/shard_map/psum | solution.py:110
  901.7 35.9 %all_gather.21 = f32[64,1024]{0,1:T(8,128)S(1)} all-gather(f32[64,32]{0,1:T(8,128)S(1)} %fusion.56), channel_id=1, replica_groups=mesh['sub'=32,'agg'=8] {'sub'}, dimensions={1}, use_global_device_ids=true | all-gather | bytes 270336 | tf_op jit(solution)/shard_map/all_gather | solution.py:114
  938.7 26.7 %all_to_all.56 = f32[8,1,3072]{2,1,0:T(1,128)S(1)} all-to-all(f32[8,1,3072]{2,1,0:T(1,128)S(1)} %reshape.680), channel_id=1, replica_groups=mesh['sub'=32,'agg'=8] {'agg'}, dimensions={0} | all-to-all | bytes 196608 | tf_op jit(solution)/shard_map/all_to_all | solution.py:116
  966.9 3.3 fusion.20
  972.1 2.0 collective-permute-start.35
  975.1 4.5 collective-permute-start.33
  979.6 3.6 collective-permute-start.37
  983.2 2.7 collective-permute-start.39
  997.1 2.0 multiply_reduce_fusion.40
  1000.0 240.8 %all-reduce.13.cloned.1.call-done = f32[16384]{0:T(1024)} async-done(((f32[16384]{0:T(1024)}), f32[16384]{0:T(1024)}) %all-reduce.13.cloned.1.call-update) | async-done | bytes 65552
  (350 shorter events, 144.6 us)
Async XLA Ops:
  11.5 35.6 %collective-permute-start = (f32[64,192]{1,0:T(8,128)S(1)}, f32[64,192]{1,0:T(8,128)}, u32[]{:S(2)}, u32[]{:S(2)}) collective-permute-start(f32[64,192]{1,0:T(8,128)S(1)} %get-tuple-element.2), channel_id=1, source_target_pairs={{248,0},{0,8},{8,16},{16,24},{24,32},{32,40},{40,48},{48,56},{56,6... | collective-permute-start | bytes 147464 | tf_op jit(solution)/shard_map/ppermute | solution.py:16
  13.6 29.9 %collective-permute-start.1 = (f32[64,192]{1,0:T(8,128)}, f32[64,192]{1,0:T(8,128)}, u32[]{:S(2)}, u32[]{:S(2)}) collective-permute-start(f32[64,192]{1,0:T(8,128)} %get-tuple-element.3), channel_id=1, source_target_pairs={{8,0},{16,8},{24,16},{32,24},{40,32},{48,40},{56,48},{64,56},{72,6... | collective-permute-start | bytes 147464 | tf_op jit(solution)/shard_map/ppermute | solution.py:16
  20.3 5.7 collective-permute-start.5
  20.4 8.1 collective-permute-start.6
  20.4 10.7 collective-permute-start.7
  26.0 13.9 %collective-permute-start.2 = (f32[64,192]{1,0:T(8,128)}, f32[64,192]{1,0:T(8,128)}, u32[]{:S(2)}, u32[]{:S(2)}) collective-permute-start(f32[64,192]{1,0:T(8,128)} %get-tuple-element.4), channel_id=1, source_target_pairs={{240,0},{248,8},{0,16},{8,24},{16,32},{24,40},{32,48},{40,56},{48,... | collective-permute-start | bytes 147464 | tf_op jit(solution)/shard_map/ppermute | solution.py:16
  28.4 9.6 collective-permute-start.3
  31.1 6.0 collective-permute-start.4
  60.5 8.4 collective-permute-start.11
  65.2 6.7 collective-permute-start.10
  65.2 8.3 collective-permute-start.9
  68.7 41.9 %collective-permute-start.8 = (f32[64,192]{1,0:T(8,128)S(1)}, f32[64,192]{1,0:T(8,128)S(1)}, u32[]{:S(2)}, u32[]{:S(2)}) collective-permute-start(f32[64,192]{1,0:T(8,128)S(1)} %get-tuple-element.34), channel_id=1, source_target_pairs={{248,0},{0,8},{8,16},{16,24},{24,32},{32,40},{40,48},{48,56},{56,6... | collective-permute-start | bytes 147464 | tf_op jit(solution)/shard_map/ppermute | solution.py:16
  68.8 39.0 %collective-permute-start.15 = (f32[64,192]{1,0:T(8,128)S(1)}, f32[64,192]{1,0:T(8,128)S(1)}, u32[]{:S(2)}, u32[]{:S(2)}) collective-permute-start(f32[64,192]{1,0:T(8,128)S(1)} %get-tuple-element.35), channel_id=1, source_target_pairs={{32,0},{40,8},{48,16},{56,24},{64,32},{72,40},{80,48},{88,56},{96,... | collective-permute-start | bytes 147464 | tf_op jit(solution)/shard_map/ppermute | solution.py:16
  68.9 35.2 %collective-permute-start.14 = (f32[64,192]{1,0:T(8,128)S(1)}, f32[64,192]{1,0:T(8,128)}, u32[]{:S(2)}, u32[]{:S(2)}) collective-permute-start(f32[64,192]{1,0:T(8,128)S(1)} %get-tuple-element.36), channel_id=1, source_target_pairs={{224,0},{232,8},{240,16},{248,24},{0,32},{8,40},{16,48},{24,56},{3... | collective-permute-start | bytes 147464 | tf_op jit(solution)/shard_map/ppermute | solution.py:16
  72.0 28.5 %collective-permute-start.13 = (f32[64,192]{1,0:T(8,128)S(1)}, f32[64,192]{1,0:T(8,128)}, u32[]{:S(2)}, u32[]{:S(2)}) collective-permute-start(f32[64,192]{1,0:T(8,128)S(1)} %get-tuple-element.37), channel_id=1, source_target_pairs={{24,0},{32,8},{40,16},{48,24},{56,32},{64,40},{72,48},{80,56},{88,... | collective-permute-start | bytes 147464 | tf_op jit(solution)/shard_map/ppermute | solution.py:16
  73.5 23.3 %collective-permute-start.12 = (f32[64,192]{1,0:T(8,128)S(1)}, f32[64,192]{1,0:T(8,128)}, u32[]{:S(2)}, u32[]{:S(2)}) collective-permute-start(f32[64,192]{1,0:T(8,128)S(1)} %get-tuple-element.38), channel_id=1, source_target_pairs={{232,0},{240,8},{248,16},{0,24},{8,32},{16,40},{24,48},{32,56},{40... | collective-permute-start | bytes 147464 | tf_op jit(solution)/shard_map/ppermute | solution.py:16
  76.6 42.9 %all-to-all-start.1 = ((s32[8,48,1]{1,2,0:T(1,128)}), s32[8,48,1]{1,2,0:T(1,128)}, u32[]{:S(2)}, u32[]{:S(2)}) async-start(s32[8,48,1]{1,2,0:T(1,128)} %bitcast.111), calls=%async_computation.1 | async-start | bytes 8192 | tf_op jit(solution)/shard_map/all_to_all | solution.py:77
  119.5 9.9 all-to-all-start
  124.3 150.4 %all-reduce.7.cloned.1.call-start = ((), (), s32[]{:S(2)}) async-start(), calls=%async_computation.5 | async-start | bytes 524288 | tf_op jit(solution)/shard_map/psum | solution.py:110
  136.3 504.1 %all-reduce.11.cloned.1.call-start = ((), (), s32[]{:S(2)}) async-start(), calls=%async_computation.7 | async-start | bytes 131072
  357.3 11.3 collective-permute-start.19
  359.3 9.3 collective-permute-start.18
  360.3 11.0 collective-permute-start.17
  364.8 20.5 %collective-permute-start.20 = (f32[64,192]{1,0:T(8,128)}, f32[64,192]{1,0:T(8,128)}, u32[]{:S(2)}, u32[]{:S(2)}) collective-permute-start(f32[64,192]{1,0:T(8,128)} %get-tuple-element.30), channel_id=1, source_target_pairs={{232,0},{240,8},{248,16},{0,24},{8,32},{16,40},{24,48},{32,56},{40... | collective-permute-start | bytes 147464 | tf_op jit(solution)/shard_map/ppermute | solution.py:16
  364.8 22.3 %collective-permute-start.21 = (f32[64,192]{1,0:T(8,128)}, f32[64,192]{1,0:T(8,128)}, u32[]{:S(2)}, u32[]{:S(2)}) collective-permute-start(f32[64,192]{1,0:T(8,128)} %get-tuple-element.29), channel_id=1, source_target_pairs={{24,0},{32,8},{40,16},{48,24},{56,32},{64,40},{72,48},{80,56},{88,... | collective-permute-start | bytes 147464 | tf_op jit(solution)/shard_map/ppermute | solution.py:16
  368.6 20.4 %collective-permute-start.22 = (f32[64,192]{1,0:T(8,128)}, f32[64,192]{1,0:T(8,128)}, u32[]{:S(2)}, u32[]{:S(2)}) collective-permute-start(f32[64,192]{1,0:T(8,128)} %get-tuple-element.28), channel_id=1, source_target_pairs={{224,0},{232,8},{240,16},{248,24},{0,32},{8,40},{16,48},{24,56},{3... | collective-permute-start | bytes 147464 | tf_op jit(solution)/shard_map/ppermute | solution.py:16
  368.6 22.2 %collective-permute-start.23 = (f32[64,192]{1,0:T(8,128)}, f32[64,192]{1,0:T(8,128)}, u32[]{:S(2)}, u32[]{:S(2)}) collective-permute-start(f32[64,192]{1,0:T(8,128)} %get-tuple-element.27), channel_id=1, source_target_pairs={{32,0},{40,8},{48,16},{56,24},{64,32},{72,40},{80,48},{88,56},{96,... | collective-permute-start | bytes 147464 | tf_op jit(solution)/shard_map/ppermute | solution.py:16
  371.3 21.3 %collective-permute-start.16 = (f32[64,192]{1,0:T(8,128)}, f32[64,192]{1,0:T(8,128)}, u32[]{:S(2)}, u32[]{:S(2)}) collective-permute-start(f32[64,192]{1,0:T(8,128)} %get-tuple-element.26), channel_id=1, source_target_pairs={{248,0},{0,8},{8,16},{16,24},{24,32},{32,40},{40,48},{48,56},{56,6... | collective-permute-start | bytes 147464 | tf_op jit(solution)/shard_map/ppermute | solution.py:16
  399.5 500.9 %all-reduce.9.cloned.1.call-start = ((), (), s32[]{:S(2)}) async-start(), calls=%async_computation.6 | async-start | bytes 524288 | tf_op jit(solution)/shard_map/psum | solution.py:110
  647.9 10.3 collective-permute-start.27
  649.6 8.7 collective-permute-start.26
  650.9 10.0 collective-permute-start.25
  654.6 6.9 collective-permute-start.28
  654.6 8.7 collective-permute-start.29
  658.2 7.0 collective-permute-start.30
  658.2 8.8 collective-permute-start.31
  660.9 7.9 collective-permute-start.24
  670.6 295.7 %copy-start.53 = (s32[128]{0:T(128)S(1)}, s32[128]{0:T(128)}, u32[]{:S(2)}) copy-start(s32[128]{0:T(128)} %multiply_add_fusion.1) | copy-start | bytes 1540
  763.4 477.4 %all-reduce.13.cloned.1.call-start = ((), (), s32[]{:S(2)}) async-start(), calls=%async_computation.8 | async-start | bytes 131072
  972.1 11.0 collective-permute-start.35
  974.1 9.1 collective-permute-start.34
  975.1 10.8 collective-permute-start.33
  979.6 8.5 collective-permute-start.36
  979.6 10.3 collective-permute-start.37
  983.1 8.5 collective-permute-start.38
  983.2 10.3 collective-permute-start.39
  985.8 9.5 collective-permute-start.32
  991.7 250.2 %copy-start.55 = (f32[64]{0:T(128)S(1)}, f32[64]{0:T(128)}, u32[]{:S(2)}) copy-start(f32[64]{0:T(128)} %copy-done.54) | copy-start | bytes 772
  (57 other events, 3702.5 us)
Sparse Core Ops, SparseCore 0:
  136.5 138.1 all-reduce.6
  399.6 240.7 all-reduce.10
  763.5 136.8 all-reduce.8
  1000.2 240.6 all-reduce.12
